TPU v7x, 32 devices: a whole 2x2x4 slice. The times are simulated.
32 devices in a mesh: fsdp: 4 (over z), tensor: 8 (over y, x, core).
Axes of the slice: x: 2, y: 2, z: 4, core: 2. Of those that a mesh axis runs over, the one named last changes fastest.
Arguments:
- tokens: bfloat16 [5120, 2048], P(('fsdp', 'tensor')), may hold values from -6 to 6
- gain_attn: bfloat16 [2048], replicated, may hold values from 0.099609375 to 1.8984375
- gain_mlp: bfloat16 [2048], replicated, may hold values from 0.099609375 to 1.8984375
- w_query: bfloat16 [2048, 2048], P('fsdp', 'tensor'), may hold values from -0.125 to 0.125
- w_key: bfloat16 [2048, 2048], P('fsdp', 'tensor'), may hold values from -0.125 to 0.125
- w_value: bfloat16 [2048, 2048], P('fsdp', 'tensor'), may hold values from -0.125 to 0.125
- w_out: bfloat16 [2048, 2048], P('tensor', 'fsdp'), may hold values from -0.5 to 0.5
- w_gate: bfloat16 [2048, 8192], P('fsdp', 'tensor'), may hold values from -0.125 to 0.125
- w_up: bfloat16 [2048, 8192], P('fsdp', 'tensor'), may hold values from -0.125 to 0.125
- w_down: bfloat16 [8192, 2048], P('tensor', 'fsdp'), may hold values from -0.09375 to 0.09375
- segment_ids: int32 [4, 1280], P('fsdp'), may hold values from 0 to 3, never falling along the last dimension, each value on 1 to 512 neighbouring positions
- out_grad: bfloat16 [5120, 2048], P(('fsdp', 'tensor')), may hold values from -6 to 6
Outputs:
- output: bfloat16 [5120, 2048], P(('fsdp', 'tensor'))
- tokens_grad: bfloat16 [5120, 2048], P(('fsdp', 'tensor'))
- gain_attn_grad: float32 [2048], replicated
- gain_mlp_grad: float32 [2048], replicated
- w_query_grad: float32 [2048, 2048], P('fsdp', 'tensor')
- w_key_grad: float32 [2048, 2048], P('fsdp', 'tensor')
- w_value_grad: float32 [2048, 2048], P('fsdp', 'tensor')
- w_out_grad: float32 [2048, 2048], P('tensor', 'fsdp')
- w_gate_grad: float32 [2048, 8192], P('fsdp', 'tensor')
- w_up_grad: float32 [2048, 8192], P('fsdp', 'tensor')
- w_down_grad: float32 [8192, 2048], P('tensor', 'fsdp')
Inputs may be any that keep to these rules, and one draw needn't show every extreme that they name: `segment_ids`: in each packed row the ids never fall; each sample has 1 to 512 tokens, and some sample in each row has exactly 512.
All inputs are finite; a program needn't handle non-finite values.
Results may differ from a plain program's by a relative error of at most 0.019.
Values may be sent and summed in bfloat16 or wider, within the bound.
A program may use at most 192 MiB of HBM per device.

v0:
```python
import math
import jax
import jax.numpy as jnp
from jax import lax
from jax.sharding import PartitionSpec as P

HEAD = 64
eps = 1e-05
rope_base = 130000.0


def dot_nt(left, right):
    return lax.dot_general(
        left, right, (((1,), (1,)), ((), ())), preferred_element_type=jnp.float32
    )


def dot_tn(left, right):
    return lax.dot_general(
        left, right, (((0,), (0,)), ((), ())), preferred_element_type=jnp.float32
    )


def rope_tables(segments):
    length = segments.shape[1]
    index = jnp.arange(length, dtype=jnp.int32)[None, :]
    change = jnp.concatenate(
        [jnp.ones((segments.shape[0], 1), dtype=bool), segments[:, 1:] != segments[:, :-1]], axis=1
    )
    start = lax.cummax(jnp.where(change, index, 0), axis=1)
    position = (index - start).astype(jnp.float32)
    half = jnp.arange(HEAD // 2, dtype=jnp.float32)
    inverse = jnp.exp(half * (-2.0 / HEAD) * math.log(rope_base))
    angle = position[:, :, None, None] * inverse[None, None, None, :]
    return (jnp.cos(angle), jnp.sin(angle))


def rotate(value, cosine, sine):
    half = value.shape[-1] // 2
    first = value[..., :half]
    second = value[..., half:]
    return jnp.concatenate(
        [first * cosine - second * sine, second * cosine + first * sine], axis=-1
    )


def norm_forward(value, gain):
    scale = lax.rsqrt(jnp.mean(value * value, axis=-1, keepdims=True) + eps)
    return (value * scale * gain, scale)


def norm_backward(value, scale, gain, grad):
    scaled_grad = grad * gain
    inner = jnp.mean(value * scaled_grad, axis=-1, keepdims=True)
    back = scale * scaled_grad - value * scale * scale * scale * inner
    gain_grad = jnp.sum(grad * value * scale, axis=0)
    return (back, gain_grad)


def row_mask(segments):
    length = segments.shape[0]
    index = jnp.arange(length, dtype=jnp.int32)
    return (segments[:, None] == segments[None, :]) & (index[None, :] <= index[:, None])


def row_scores(query, key, segments):
    scores = jnp.einsum("qhd,khd->hqk", query, key, preferred_element_type=jnp.float32) * HEAD ** (
        -0.5
    )
    return jnp.where(row_mask(segments)[None, :, :], scores, -1000000000.0)


def attend_row(inputs):
    query, key, value, segments = inputs
    scores = row_scores(query, key, segments)
    top = jnp.max(scores, axis=-1, keepdims=True)
    expo = jnp.exp(scores - top)
    total = jnp.sum(expo, axis=-1, keepdims=True)
    weights = (expo / total).astype(jnp.bfloat16)
    attended = jnp.einsum("hqk,khd->qhd", weights, value, preferred_element_type=jnp.float32)
    return (attended, (top + jnp.log(total))[..., 0])


def attend_back(inputs):
    query, key, value, segments, logsum, grad_out = inputs
    scores = row_scores(query, key, segments)
    weights = jnp.exp(scores - logsum[..., None])
    grad_value = jnp.einsum(
        "hqk,qhd->khd", weights.astype(jnp.bfloat16), grad_out, preferred_element_type=jnp.float32
    )
    grad_weights = jnp.einsum("qhd,khd->hqk", grad_out, value, preferred_element_type=jnp.float32)
    inner = jnp.sum(weights * grad_weights, axis=-1, keepdims=True)
    grad_scores = (weights * (grad_weights - inner)).astype(jnp.bfloat16)
    grad_query = jnp.einsum(
        "hqk,khd->qhd", grad_scores, key, preferred_element_type=jnp.float32
    ) * HEAD ** (-0.5)
    grad_key = jnp.einsum(
        "hqk,qhd->khd", grad_scores, query, preferred_element_type=jnp.float32
    ) * HEAD ** (-0.5)
    return (grad_query, grad_key, grad_value)


def shards(
    tokens,
    gain_attn,
    gain_mlp,
    w_query,
    w_key,
    w_value,
    w_out,
    w_gate,
    w_up,
    w_down,
    segment_ids,
    out_grad,
):
    rows_grp = segment_ids.shape[0]
    row_len = segment_ids.shape[1]
    local = (w_query, w_key, w_value, w_out, w_gate, w_up, w_down)
    gathered = (
        lax.all_gather(local[0], "fsdp", axis=0, tiled=True),
        lax.all_gather(local[1], "fsdp", axis=0, tiled=True),
        lax.all_gather(local[2], "fsdp", axis=0, tiled=True),
        lax.all_gather(local[3], "fsdp", axis=1, tiled=True),
        lax.all_gather(local[4], "fsdp", axis=0, tiled=True),
        lax.all_gather(local[5], "fsdp", axis=0, tiled=True),
        lax.all_gather(local[6], "fsdp", axis=1, tiled=True),
    )
    wq, wk, wv, wo, wg, wu, wd = gathered
    heads_dev = wq.shape[1] // HEAD
    group = rows_grp * row_len
    gain_a = gain_attn.astype(jnp.float32)
    gain_m = gain_mlp.astype(jnp.float32)
    cosine, sine = rope_tables(segment_ids)

    def heads(value):
        return value.reshape(rows_grp, row_len, heads_dev, HEAD)

    x = tokens.astype(jnp.float32)
    normed_local, scale_a = norm_forward(x, gain_a)
    normed_a = lax.all_gather(normed_local.astype(jnp.bfloat16), "tensor", axis=0, tiled=True)
    query = rotate(
        heads(jnp.dot(normed_a, wq, preferred_element_type=jnp.float32)), cosine, sine
    ).astype(jnp.bfloat16)
    key = rotate(
        heads(jnp.dot(normed_a, wk, preferred_element_type=jnp.float32)), cosine, sine
    ).astype(jnp.bfloat16)
    value = heads(jnp.dot(normed_a, wv, preferred_element_type=jnp.float32).astype(jnp.bfloat16))
    attended, logsum = lax.map(attend_row, (query, key, value, segment_ids))
    attended = attended.reshape(group, heads_dev * HEAD).astype(jnp.bfloat16)
    hidden = x + lax.psum_scatter(
        jnp.dot(attended, wo, preferred_element_type=jnp.float32),
        "tensor",
        scatter_dimension=0,
        tiled=True,
    )
    normed_hidden, scale_m = norm_forward(hidden, gain_m)
    normed_m = lax.all_gather(normed_hidden.astype(jnp.bfloat16), "tensor", axis=0, tiled=True)
    gate = jnp.dot(normed_m, wg, preferred_element_type=jnp.float32)
    up = jnp.dot(normed_m, wu, preferred_element_type=jnp.float32)
    sigma = jax.nn.sigmoid(gate)
    silu_gate = gate * sigma
    act = (silu_gate * up).astype(jnp.bfloat16)
    output = hidden + lax.psum_scatter(
        jnp.dot(act, wd, preferred_element_type=jnp.float32).astype(jnp.bfloat16),
        "tensor",
        scatter_dimension=0,
        tiled=True,
    ).astype(jnp.float32)
    wq, wk, wv, wo, wg, wu, wd = (
        lax.all_gather(local[0], "fsdp", axis=0, tiled=True),
        lax.all_gather(local[1], "fsdp", axis=0, tiled=True),
        lax.all_gather(local[2], "fsdp", axis=0, tiled=True),
        lax.all_gather(local[3], "fsdp", axis=1, tiled=True),
        lax.all_gather(local[4], "fsdp", axis=0, tiled=True),
        lax.all_gather(local[5], "fsdp", axis=0, tiled=True),
        lax.all_gather(local[6], "fsdp", axis=1, tiled=True),
    )
    grad_all = lax.all_gather(out_grad, "tensor", axis=0, tiled=True)
    grad_down = dot_tn(act, grad_all)
    grad_act = dot_nt(grad_all, wd)
    grad_gate = (grad_act * up * (sigma * (1.0 + gate * (1.0 - sigma)))).astype(jnp.bfloat16)
    grad_up = (grad_act * silu_gate).astype(jnp.bfloat16)
    grad_wgate = dot_tn(normed_m, grad_gate)
    grad_wup = dot_tn(normed_m, grad_up)
    grad_nm = lax.psum_scatter(
        dot_nt(grad_gate, wg) + dot_nt(grad_up, wu), "tensor", scatter_dimension=0, tiled=True
    )
    back_m, gain_m_part = norm_backward(hidden, scale_m, gain_m, grad_nm)
    grad_hidden = out_grad.astype(jnp.float32) + back_m
    grad_hidden_low = grad_hidden.astype(jnp.bfloat16)
    branch_all = lax.all_gather(grad_hidden_low, "tensor", axis=0, tiled=True)
    grad_wout = dot_tn(attended, branch_all)
    grad_attended = heads(dot_nt(branch_all, wo).astype(jnp.bfloat16))
    grad_query, grad_key, grad_value = lax.map(
        attend_back, (query, key, value, segment_ids, logsum, grad_attended)
    )
    grad_qpre = (
        rotate(grad_query, cosine, -sine).reshape(group, heads_dev * HEAD).astype(jnp.bfloat16)
    )
    grad_kpre = (
        rotate(grad_key, cosine, -sine).reshape(group, heads_dev * HEAD).astype(jnp.bfloat16)
    )
    grad_vpre = grad_value.reshape(group, heads_dev * HEAD).astype(jnp.bfloat16)
    grad_wq = dot_tn(normed_a, grad_qpre)
    grad_wk = dot_tn(normed_a, grad_kpre)
    grad_wv = dot_tn(normed_a, grad_vpre)
    grad_na_part = dot_nt(grad_qpre, wq) + dot_nt(grad_kpre, wk) + dot_nt(grad_vpre, wv)
    grad_na = lax.psum_scatter(
        grad_na_part.astype(jnp.bfloat16), "tensor", scatter_dimension=0, tiled=True
    ).astype(jnp.float32)
    back_a, gain_a_part = norm_backward(x, scale_a, gain_a, grad_na)
    tokens_grad = (grad_hidden + back_a).astype(jnp.bfloat16)
    gain_a_grad, gain_m_grad = lax.psum((gain_a_part, gain_m_part), ("fsdp", "tensor"))
    weight_grads = (
        lax.psum_scatter(
            grad_wq.astype(jnp.bfloat16), "fsdp", scatter_dimension=0, tiled=True
        ).astype(jnp.float32),
        lax.psum_scatter(
            grad_wk.astype(jnp.bfloat16), "fsdp", scatter_dimension=0, tiled=True
        ).astype(jnp.float32),
        lax.psum_scatter(
            grad_wv.astype(jnp.bfloat16), "fsdp", scatter_dimension=0, tiled=True
        ).astype(jnp.float32),
        lax.psum_scatter(
            grad_wout.astype(jnp.bfloat16), "fsdp", scatter_dimension=1, tiled=True
        ).astype(jnp.float32),
        lax.psum_scatter(
            grad_wgate.astype(jnp.bfloat16), "fsdp", scatter_dimension=0, tiled=True
        ).astype(jnp.float32),
        lax.psum_scatter(
            grad_wup.astype(jnp.bfloat16), "fsdp", scatter_dimension=0, tiled=True
        ).astype(jnp.float32),
        lax.psum_scatter(
            grad_down.astype(jnp.bfloat16), "fsdp", scatter_dimension=1, tiled=True
        ).astype(jnp.float32),
    )
    return (
        output.astype(jnp.bfloat16),
        tokens_grad,
        gain_a_grad,
        gain_m_grad,
        weight_grads[0],
        weight_grads[1],
        weight_grads[2],
        weight_grads[3],
        weight_grads[4],
        weight_grads[5],
        weight_grads[6],
    )


def solution(mesh):
    return jax.shard_map(
        shards,
        mesh=mesh,
        in_specs=(
            P(("fsdp", "tensor"), None),
            P(),
            P(),
            P("fsdp", "tensor"),
            P("fsdp", "tensor"),
            P("fsdp", "tensor"),
            P("tensor", "fsdp"),
            P("fsdp", "tensor"),
            P("fsdp", "tensor"),
            P("tensor", "fsdp"),
            P("fsdp", None),
            P(("fsdp", "tensor"), None),
        ),
        out_specs=(
            P(("fsdp", "tensor"), None),
            P(("fsdp", "tensor"), None),
            P(),
            P(),
            P("fsdp", "tensor"),
            P("fsdp", "tensor"),
            P("fsdp", "tensor"),
            P("tensor", "fsdp"),
            P("fsdp", "tensor"),
            P("fsdp", "tensor"),
            P("tensor", "fsdp"),
        ),
        check_vma=False,
    )
```

profile of v0, /device:TPU:0, one launch (start us, length us, event | category | flops | bytes accessed | tf_op | source)
XLA Modules:
  0.0 1231.1 jit_solution(9686080261791631921)
XLA Ops:
  10.5 2.1 fusion.18
  17.1 1.8 fusion.7
  20.3 20.0 %all-gather.18.cloned.1.call-done = bf16[2048,256]{1,0:T(8,128)(2,1)} async-done(((bf16[512,256]{1,0:T(8,128)(2,1)}), bf16[2048,256]{1,0:T(8,128)(2,1)}) %all-gather.18.cloned.1.call-update) | async-done | bytes 1048592 | tf_op jit(solution)/shard_map/all_gather | solution.py:122
  40.3 43.0 %all-gather.12.cloned.1.call-done = bf16[1280,2048]{1,0:T(8,128)(2,1)} async-done(((bf16[160,2048]{1,0:T(8,128)(2,1)}), bf16[1280,2048]{1,0:T(8,128)(2,1)}) %all-gather.12.cloned.1.call-update) | async-done | bytes 5242896 | tf_op jit(solution)/shard_map/all_gather | solution.py:141
  83.3 4.3 fusion.41
  87.7 25.2 %all-gather.16.cloned.1.call-done = bf16[2048,256]{1,0:T(8,128)(2,1)} async-done(((bf16[512,256]{1,0:T(8,128)(2,1)}), bf16[2048,256]{1,0:T(8,128)(2,1)}) %all-gather.16.cloned.1.call-update) | async-done | bytes 1048592 | tf_op jit(solution)/shard_map/all_gather | solution.py:121
  112.9 4.3 fusion.40
  117.6 11.1 fusion.39
  128.8 10.6 fusion.1
  139.4 2.4 all-gather.14.cloned.1.call-done
  141.8 4.3 convolution_convert_fusion.9
  146.1 21.8 %fusion.14 = bf16[4,64,1280]{2,1,0:T(8,128)(2,1)S(1)} fusion(bf16[1280,4,64]{0,2,1:T(8,128)(2,1)S(1)} %bitcast.97, f32[4,1280,1280]{1,2,0:T(8,128)} %get-tuple-element.91, f32[4,1280]{1,0:T(4,128)S(1)} %fusion.1, f32[4,1280]{1,0:T(4,128)S(1)} %get-tuple-element.90), kind=kOutput, calls=%fused_computation.41 | convolution fusion | flops 858849280 | bytes 27566080 | tf_op jit(solution)/shard_map/while/body/eval_jaxpr/hqk,khd->qhd/dot_general | solution.py:80
  167.9 2.8 all-gather.20.cloned.1.call-done
  170.6 6.7 fusion.42
  178.2 80.4 %reduce-scatter.12.cloned.1.call-done = f32[160,2048]{1,0:T(8,128)} async-done(((f32[1280,2048]{1,0:T(8,128)}), f32[160,2048]{1,0:T(8,128)}) %reduce-scatter.12.cloned.1.call-update) | async-done | bytes 1310736 | tf_op jit(solution)/shard_map/reduce_scatter | solution.py:151
  258.6 1.6 multiply_reduce_fusion.3
  263.3 77.6 %all-gather.26.cloned.1.call-done = bf16[2048,1024]{1,0:T(8,128)(2,1)} async-done(((bf16[512,1024]{1,0:T(8,128)(2,1)}), bf16[2048,1024]{1,0:T(8,128)(2,1)}) %all-gather.26.cloned.1.call-update) | async-done | bytes 4194320 | tf_op jit(solution)/shard_map/all_gather | solution.py:126
  340.9 42.1 %all-gather.22.cloned.1.call-done = bf16[1280,2048]{1,0:T(8,128)(2,1)} async-done(((bf16[160,2048]{1,0:T(8,128)(2,1)}), bf16[1280,2048]{1,0:T(8,128)(2,1)}) %all-gather.22.cloned.1.call-update) | async-done | bytes 5242896 | tf_op jit(solution)/shard_map/all_gather | solution.py:158
  383.0 10.2 fusion.44
  393.3 72.2 %all-gather.24.cloned.1.call-done = bf16[2048,1024]{1,0:T(8,128)(2,1)} async-done(((bf16[512,1024]{1,0:T(8,128)(2,1)}), bf16[2048,1024]{1,0:T(8,128)(2,1)}) %all-gather.24.cloned.1.call-update) | async-done | bytes 4194320 | tf_op jit(solution)/shard_map/all_gather | solution.py:125
  465.4 10.2 fusion.43
  475.6 70.5 %all-gather.28.cloned.1.call-done = bf16[1024,2048]{1,0:T(8,128)(2,1)} async-done(((bf16[1024,512]{1,0:T(8,128)(2,1)}), bf16[1024,2048]{1,0:T(8,128)(2,1)}) %all-gather.28.cloned.1.call-update) | async-done | bytes 4194320 | tf_op jit(solution)/shard_map/all_gather | solution.py:127
  546.2 41.6 %all-gather.30.cloned.1.call-done = bf16[1280,2048]{1,0:T(8,128)(2,1)} async-done(((bf16[160,2048]{1,0:T(8,128)(2,1)}), bf16[1280,2048]{1,0:T(8,128)(2,1)}) %all-gather.30.cloned.1.call-update) | async-done | bytes 5242896 | tf_op jit(solution)/shard_map/all_gather | solution.py:179
  587.7 14.7 %multiply_convert_fusion.1 = (bf16[1280,1024]{1,0:T(8,128)(2,1)S(1)}, bf16[1280,1024]{1,0:T(8,128)(2,1)S(1)}, bf16[1280,1024]{1,0:T(8,128)(2,1)}) fusion(f32[1280,1024]{1,0:T(8,128)} %fusion.43, f32[1280,1024]{1,0:T(8,128)} %fusion.44, bf16[1280,2048]{1,0:T(8,128)(2,1)} %all-gather.30.cloned.1.call-done, bf16[1024,2048]{1,0:T(8,128)(2,1)} %all-gather.28.cloned.1.call-done), kind=kOutput, calls=%fused_computation.17 | convolution fusion | flops 5388369920 | bytes 27787264 | tf_op jit(solution)/shard_map/dot_general | solution.py:13
  602.4 8.2 fusion.45
  610.7 11.0 convolution_add_fusion
  621.7 81.7 %reduce-scatter.16.cloned.1.call-done = f32[160,2048]{1,0:T(8,128)} async-done(((f32[1280,2048]{1,0:T(8,128)}), f32[160,2048]{1,0:T(8,128)}) %reduce-scatter.16.cloned.1.call-update) | async-done | bytes 1310736 | tf_op jit(solution)/shard_map/reduce_scatter | solution.py:186
  703.4 1.7 multiply_reduce_fusion.1
  705.1 2.6 fusion.38
  707.8 10.1 convolution_convert_fusion.1
  718.0 10.2 convolution_convert_fusion.2
  728.2 10.2 convolution_convert_fusion.3
  738.9 10.1 all-gather.32.cloned.1.call-done
  749.0 5.0 convolution_convert_fusion.4
  754.1 4.3 convolution_convert_fusion.8
  758.4 10.8 fusion.11
  769.2 5.1 convolution_convert_fusion.5
  774.3 16.7 %multiply_reduce_fusion = (f32[4,1280]{1,0:T(4,128)S(1)}, f32[4,1280,1280]{1,2,0:T(8,128)}) fusion(f32[4,1280,1280]{1,2,0:T(8,128)} %get-tuple-element.91, f32[4,1280]{1,0:T(4,128)S(1)} %log_add_fusion, bf16[1280,4,64]{0,2,1:T(8,128)(2,1)S(1)} %bitcast.90, bf16[1280,4,64]{0,2,1:T(8,128)(2,1)S(1)} %bitcast.98), kind=kOutput, calls=%fused_computation.3 | convolution fusion | flops 858516480 | bytes 53780480 | tf_op jit(solution)/shard_map/while/body/eval_jaxpr/qhd,khd->hqk/dot_general | solution.py:91
  791.2 22.5 %multiply_convert_fusion = bf16[4,1280,1280]{1,2,0:T(8,128)(2,1)} fusion(f32[4,1280,1280]{1,2,0:T(8,128)} %get-tuple-element.93, f32[4,1280,1280]{1,2,0:T(8,128)} %get-tuple-element.91, f32[4,1280]{1,0:T(4,128)S(1)} %get-tuple-element.92, f32[4,1280]{1,0:T(4,128)S(1)} %log_add_fusion), kind=kLoop, calls=%fused_computation.2 | loop fusion | flops 26214400 | bytes 65576960 | tf_op jit(solution)/shard_map/while/body/eval_jaxpr/convert_element_type | solution.py:93
  813.7 9.0 fusion.10
  822.8 7.2 fusion.9
  830.5 2.6 convolution_convert_fusion.6
  833.2 5.1 convolution_convert_fusion.7
  838.6 2.9 fusion.46
  841.5 5.6 fusion.47
  847.1 8.4 add_convert_fusion
  855.6 10.0 convolution_convert_fusion
  865.7 2.9 convert_element_type.194
  868.5 39.0 %reduce-scatter.30.cloned.1.call-done = bf16[512,1024]{1,0:T(8,128)(2,1)} async-done(((bf16[2048,1024]{1,0:T(8,128)(2,1)}), bf16[512,1024]{1,0:T(8,128)(2,1)}) %reduce-scatter.30.cloned.1.call-update) | async-done | bytes 1048592 | tf_op jit(solution)/shard_map/reduce_scatter | solution.py:231
  907.5 2.8 convert_element_type.192
  910.3 76.6 %reduce-scatter.28.cloned.1.call-done = bf16[512,1024]{1,0:T(8,128)(2,1)} async-done(((bf16[2048,1024]{1,0:T(8,128)(2,1)}), bf16[512,1024]{1,0:T(8,128)(2,1)}) %reduce-scatter.28.cloned.1.call-update) | async-done | bytes 1048592 | tf_op jit(solution)/shard_map/reduce_scatter | solution.py:228
  986.9 2.8 convert_element_type.190
  989.7 27.2 %reduce-scatter.26.cloned.1.call-done = bf16[256,512]{1,0:T(8,128)(2,1)} async-done(((bf16[256,2048]{1,0:T(8,128)(2,1)}), bf16[256,512]{1,0:T(8,128)(2,1)}) %reduce-scatter.26.cloned.1.call-update) | async-done | bytes 262160 | tf_op jit(solution)/shard_map/reduce_scatter | solution.py:225
  1016.9 1.8 convert_element_type.188
  1018.7 26.1 %reduce-scatter.24.cloned.1.call-done = bf16[512,256]{1,0:T(8,128)(2,1)} async-done(((bf16[2048,256]{1,0:T(8,128)(2,1)}), bf16[512,256]{1,0:T(8,128)(2,1)}) %reduce-scatter.24.cloned.1.call-update) | async-done | bytes 262160 | tf_op jit(solution)/shard_map/reduce_scatter | solution.py:222
  1044.8 1.8 convert_element_type.186
  1046.6 26.5 %reduce-scatter.22.cloned.1.call-done = bf16[512,256]{1,0:T(8,128)(2,1)} async-done(((bf16[2048,256]{1,0:T(8,128)(2,1)}), bf16[512,256]{1,0:T(8,128)(2,1)}) %reduce-scatter.22.cloned.1.call-update) | async-done | bytes 262160 | tf_op jit(solution)/shard_map/reduce_scatter | solution.py:219
  1073.1 1.8 convert_element_type.184
  1074.9 26.2 %reduce-scatter.20.cloned.1.call-done = bf16[512,256]{1,0:T(8,128)(2,1)} async-done(((bf16[2048,256]{1,0:T(8,128)(2,1)}), bf16[512,256]{1,0:T(8,128)(2,1)}) %reduce-scatter.20.cloned.1.call-update) | async-done | bytes 262160 | tf_op jit(solution)/shard_map/reduce_scatter | solution.py:216
  1101.0 1.8 convert_element_type.182
  1102.8 57.3 %reduce-scatter.18.cloned.1.call-done = bf16[160,2048]{1,0:T(8,128)(2,1)} async-done(((bf16[1280,2048]{1,0:T(8,128)(2,1)}), bf16[160,2048]{1,0:T(8,128)(2,1)}) %reduce-scatter.18.cloned.1.call-update) | async-done | bytes 655376 | tf_op jit(solution)/shard_map/reduce_scatter | solution.py:209
  1161.6 39.8 %all-reduce = (f32[2048]{0:T(1024)}, f32[2048]{0:T(1024)}) all-reduce(f32[2048]{0:T(1024)S(1)} %get-tuple-element.54, f32[2048]{0:T(1024)S(1)} %get-tuple-element.52), channel_id=1, replica_groups=mesh['fsdp'=4,'tensor'=8] {'fsdp','tensor'}, use_global_device_ids=true, to_apply=%region_14.15 | all-reduce | flops 4096 | bytes 32768 | tf_op jit(solution)/shard_map/psum | solution.py:214
  1201.4 19.3 %reduce-scatter.14.cloned.1.call-done = bf16[160,2048]{1,0:T(8,128)(2,1)} async-done(((bf16[1280,2048]{1,0:T(8,128)(2,1)}), bf16[160,2048]{1,0:T(8,128)(2,1)}) %reduce-scatter.14.cloned.1.call-update) | async-done | bytes 655376 | tf_op jit(solution)/shard_map/reduce_scatter | solution.py:164
  1220.7 3.4 fusion.23
  (127 shorter events, 16.7 us)
Async XLA Ops:
  7.2 33.1 %all-gather.18.cloned.1.call-start = ((), (), s32[]{:S(2)}) async-start(), calls=%async_computation.14 | async-start | bytes 1310720 | tf_op jit(solution)/shard_map/all_gather | solution.py:122
  7.9 75.4 %all-gather.12.cloned.1.call-start = ((), (), s32[]{:S(2)}) async-start(), calls=%async_computation.11 | async-start | bytes 5898240 | tf_op jit(solution)/shard_map/all_gather | solution.py:141
  8.6 1.3 copy-start.17
  10.0 0.6 copy-start.19
  12.7 100.2 %all-gather.16.cloned.1.call-start = ((), (), s32[]{:S(2)}) async-start(), calls=%async_computation.13 | async-start | bytes 1310720 | tf_op jit(solution)/shard_map/all_gather | solution.py:121
  13.4 128.3 %all-gather.14.cloned.1.call-start = ((), (), s32[]{:S(2)}) async-start(), calls=%async_computation.12 | async-start | bytes 1310720 | tf_op jit(solution)/shard_map/all_gather | solution.py:123
  14.0 156.6 %all-gather.20.cloned.1.call-start = ((), (), s32[]{:S(2)}) async-start(), calls=%async_computation.15 | async-start | bytes 1310720 | tf_op jit(solution)/shard_map/all_gather | solution.py:124
  14.6 243.9 %reduce-scatter.12.cloned.1.call-start = ((), (), s32[]{:S(2)}) async-start(), calls=%async_computation.16 | async-start | bytes 11796480 | tf_op jit(solution)/shard_map/reduce_scatter | solution.py:151
  20.3 97.0 %copy-start.4 = (f32[1280,32]{0,1:T(8,128)}, f32[1280,32]{0,1:T(8,128)S(1)}, u32[]{:S(2)}) copy-start(f32[1280,32]{0,1:T(8,128)S(1)} %get-tuple-element.89) | copy-start | bytes 491524
  117.6 11.1 copy-start.6
  117.6 11.1 copy-start.8
  117.6 11.1 copy-start.10
  117.6 11.1 copy-start.12
  177.3 0.8 copy-start.21
  177.3 81.2 %copy-start = (bf16[160,2048]{1,0:T(8,128)(2,1)S(1)}, bf16[160,2048]{1,0:T(8,128)(2,1)}, u32[]{:S(2)}) copy-start(bf16[160,2048]{1,0:T(8,128)(2,1)} %param.12) | copy-start | bytes 1966084
  177.4 163.5 %all-gather.26.cloned.1.call-start = ((), (), s32[]{:S(2)}) async-start(), calls=%async_computation.19 | async-start | bytes 5242880 | tf_op jit(solution)/shard_map/all_gather | solution.py:126
  178.1 204.9 %all-gather.22.cloned.1.call-start = ((), (), s32[]{:S(2)}) async-start(), calls=%async_computation.17 | async-start | bytes 5898240 | tf_op jit(solution)/shard_map/all_gather | solution.py:158
  261.2 204.2 %all-gather.24.cloned.1.call-start = ((), (), s32[]{:S(2)}) async-start(), calls=%async_computation.18 | async-start | bytes 5242880 | tf_op jit(solution)/shard_map/all_gather | solution.py:125
  261.9 284.2 %all-gather.28.cloned.1.call-start = ((), (), s32[]{:S(2)}) async-start(), calls=%async_computation.20 | async-start | bytes 5242880 | tf_op jit(solution)/shard_map/all_gather | solution.py:127
  262.5 325.2 %all-gather.30.cloned.1.call-start = ((), (), s32[]{:S(2)}) async-start(), calls=%async_computation.22 | async-start | bytes 5898240 | tf_op jit(solution)/shard_map/all_gather | solution.py:179
  263.2 440.2 %reduce-scatter.16.cloned.1.call-start = ((), (), s32[]{:S(2)}) async-start(), calls=%async_computation.23 | async-start | bytes 11796480 | tf_op jit(solution)/shard_map/reduce_scatter | solution.py:186
  587.7 14.7 %copy-start.23 = (bf16[2048,1024]{1,0:T(8,128)(2,1)S(1)}, bf16[2048,1024]{1,0:T(8,128)(2,1)}, u32[]{:S(2)}) copy-start(bf16[2048,1024]{1,0:T(8,128)(2,1)} %all-gather.24.cloned.1.call-done) | copy-start | bytes 12582916
  602.4 8.3 copy-start.25
  602.4 8.3 copy-start.24
  602.4 8.3 copy-start.22
  621.7 83.4 %copy-start.3 = (bf16[160,2048]{1,0:T(8,128)(2,1)S(1)}, bf16[160,2048]{1,0:T(8,128)(2,1)}, u32[]{:S(2)}) copy-start(bf16[160,2048]{1,0:T(8,128)(2,1)} %param.23) | copy-start | bytes 1966084
  621.7 127.3 %all-gather.32.cloned.1.call-start = ((), (), s32[]{:S(2)}) async-start(), calls=%async_computation.24 | async-start | bytes 5898240 | tf_op jit(solution)/shard_map/all_gather | solution.py:192
  707.8 157.9 %reduce-scatter.32.cloned.1.call-start = ((), (), s32[]{:S(2)}) async-start(), calls=%async_computation.32 | async-start | bytes 5242880 | tf_op jit(solution)/shard_map/reduce_scatter | solution.py:234
  717.9 189.6 %reduce-scatter.30.cloned.1.call-start = ((), (), s32[]{:S(2)}) async-start(), calls=%async_computation.31 | async-start | bytes 5242880 | tf_op jit(solution)/shard_map/reduce_scatter | solution.py:231
  728.2 258.8 %reduce-scatter.28.cloned.1.call-start = ((), (), s32[]{:S(2)}) async-start(), calls=%async_computation.30 | async-start | bytes 5242880 | tf_op jit(solution)/shard_map/reduce_scatter | solution.py:228
  738.4 278.4 %reduce-scatter.26.cloned.1.call-start = ((), (), s32[]{:S(2)}) async-start(), calls=%async_computation.29 | async-start | bytes 1310720 | tf_op jit(solution)/shard_map/reduce_scatter | solution.py:225
  754.0 290.8 %reduce-scatter.24.cloned.1.call-start = ((), (), s32[]{:S(2)}) async-start(), calls=%async_computation.28 | async-start | bytes 1310720 | tf_op jit(solution)/shard_map/reduce_scatter | solution.py:222
  791.0 282.1 %reduce-scatter.22.cloned.1.call-start = ((), (), s32[]{:S(2)}) async-start(), calls=%async_computation.27 | async-start | bytes 1310720 | tf_op jit(solution)/shard_map/reduce_scatter | solution.py:219
  791.2 22.5 %copy-start.11 = (bf16[1280,4,32]{0,2,1:T(8,128)(2,1)S(1)}, bf16[1280,4,32]{0,2,1:T(8,128)(2,1)}, u32[]{:S(2)}) copy-start(bf16[1280,4,32]{0,2,1:T(8,128)(2,1)} %copy-done.10) | copy-start | bytes 983044
  791.2 22.5 %copy-start.13 = (bf16[1280,4,32]{0,2,1:T(8,128)(2,1)S(1)}, bf16[1280,4,32]{0,2,1:T(8,128)(2,1)}, u32[]{:S(2)}) copy-start(bf16[1280,4,32]{0,2,1:T(8,128)(2,1)} %copy-done.12) | copy-start | bytes 983044
  813.7 9.0 copy-start.7
  813.7 9.0 copy-start.9
  813.7 16.7 %slice-start = ((s8[5242880]{0:T(1024)(128)(4,1)}), s8[1048576]{0:T(1024)(128)(4,1)S(1)}, s32[]{:S(2)}) async-start(s8[5242880]{0:T(1024)(128)(4,1)} %bitcast.104), calls=%async_computation.33 | async-start | bytes 2097152
  822.7 7.3 copy-start.5
  822.7 7.3 copy-start.16
  822.8 7.7 slice-start.1
  833.1 267.9 %reduce-scatter.20.cloned.1.call-start = ((), (), s32[]{:S(2)}) async-start(), calls=%async_computation.26 | async-start | bytes 1310720 | tf_op jit(solution)/shard_map/reduce_scatter | solution.py:216
  838.3 321.8 %reduce-scatter.18.cloned.1.call-start = ((), (), s32[]{:S(2)}) async-start(), calls=%async_computation.25 | async-start | bytes 5898240 | tf_op jit(solution)/shard_map/reduce_scatter | solution.py:209
  838.5 2.9 copy-start.14
  841.5 5.6 copy-start.15
  855.5 365.1 %reduce-scatter.14.cloned.1.call-start = ((), (), s32[]{:S(2)}) async-start(), calls=%async_computation.21 | async-start | bytes 5898240 | tf_op jit(solution)/shard_map/reduce_scatter | solution.py:164
  868.5 291.6 %copy-start.1 = (bf16[160,2048]{1,0:T(8,128)(2,1)S(1)}, bf16[160,2048]{1,0:T(8,128)(2,1)}, u32[]{:S(2)}) copy-start(bf16[160,2048]{1,0:T(8,128)(2,1)} %param.12) | copy-start | bytes 1966084
  868.5 291.6 %copy-start.18 = (f32[2048]{0:T(1024)S(1)}, f32[2048]{0:T(1024)}, u32[]{:S(2)}) copy-start(f32[2048]{0:T(1024)} %copy-done.17) | copy-start | bytes 24580
  868.5 291.6 %copy-start.20 = (f32[160]{0:T(256)S(1)}, f32[160]{0:T(256)}, u32[]{:S(2)}) copy-start(f32[160]{0:T(256)} %copy-done.19) | copy-start | bytes 1924
  910.3 310.4 %copy-start.2 = (f32[160,2048]{1,0:T(8,128)S(1)}, f32[160,2048]{1,0:T(8,128)}, u32[]{:S(2)}) copy-start(f32[160,2048]{1,0:T(8,128)} %reduce-scatter.16.cloned.1.call-done) | copy-start | bytes 3932164
Sparse Core Ops, SparseCore 0:
  9.6 30.6 all-gather.17
  42.8 40.5 all-gather.11
  84.9 27.9 all-gather.15
  114.3 27.4 all-gather.13
  143.2 27.4 all-gather.19
  177.5 81.0 reduce-scatter.11
  260.1 80.7 all-gather.25
  343.4 39.6 all-gather.21
  384.6 80.7 all-gather.23
  466.8 79.2 all-gather.27
  548.0 39.6 all-gather.29
  621.8 81.5 reduce-scatter.15
  707.9 41.0 all-gather.31
  751.2 76.7 reduce-scatter.31
  830.2 77.2 reduce-scatter.29
  909.7 77.2 reduce-scatter.27
  989.2 27.6 reduce-scatter.25
  1019.0 25.7 reduce-scatter.23
  1047.2 25.8 reduce-scatter.21
  1075.2 25.7 reduce-scatter.19
  1104.8 55.2 reduce-scatter.17
  1163.5 57.1 reduce-scatter.13
where the time goes:
time: 1240 us; the launch traced here: 1230 us
  waiting for transfers between devices  873 us (70%)
  matrix products  230 us (19%)
  other arithmetic  70.7 us (6%)
  blocking collectives  39.8 us (3%)
  between operations  15 us (1%)
    reduce_scatter x1, waiting for transfers between devices, shards(): lax.psum_scatter(dot_nt(grad_gate, wg) + dot_nt(grad_up, wu), 'tensor', s...  81.7 us
    reduce_scatter x1, waiting for transfers between devices, shards(): lax.psum_scatter(jnp.dot(attended, wo, preferred_element_type=jnp.float32...  80.4 us
    all_gather x1, waiting for transfers between devices, shards(): lax.all_gather(local[5], 'fsdp', axis=0, tiled=True)  77.6 us
    reduce_scatter x1, waiting for transfers between devices, shards(): lax.psum_scatter(grad_wgate.astype(jnp.bfloat16), 'fsdp', scatter_dimensi...  76.6 us
    all_gather x1, waiting for transfers between devices, shards(): lax.all_gather(local[4], 'fsdp', axis=0, tiled=True)  72.2 us
    all_gather x1, waiting for transfers between devices, shards(): lax.all_gather(local[6], 'fsdp', axis=1, tiled=True)  70.5 us
    reduce_scatter x1, waiting for transfers between devices, shards(): lax.psum_scatter(grad_na_part.astype(jnp.bfloat16), 'tensor', scatter_dim...  57.3 us
    dot_general x7, matrix products, dot_nt(): lax.dot_general(left, right, (((1,), (1,)), ((), ())), preferred_element_...  55.2 us
  transfers between devices with their start and end apart: 22, of which 21 were waited for; matrix products, arithmetic and copies ran while one was open for 21% of the time, Pallas kernels for 0%

commit v1 on v0

--- a/solution.py
+++ b/solution.py
@@ -7,6 +7,24 @@
 HEAD = 64
 eps = 1e-05
 rope_base = 130000.0
+
+
+def joined_along(parts, dim):
+    lengths = list(parts.shape[1:])
+    lengths[dim] *= parts.shape[0]
+    return jnp.moveaxis(parts, 0, dim).reshape(lengths)
+
+
+def grow_blocks(x, axis):
+    size = lax.axis_size(axis)
+    blocks = x[None]
+    for level in range(size.bit_length() - 1):
+        stride = 1 << level
+        other = lax.ppermute(blocks, axis, [(i, i ^ stride) for i in range(size)])
+        both = jnp.stack([blocks, other])
+        upper = lax.axis_index(axis) >> level & 1
+        blocks = jnp.where(upper == 0, both, both[::-1]).reshape(-1, *x.shape)
+    return blocks
 
 
 def dot_nt(left, right):
@@ -176,7 +194,7 @@
         lax.all_gather(local[5], "fsdp", axis=0, tiled=True),
         lax.all_gather(local[6], "fsdp", axis=1, tiled=True),
     )
-    grad_all = lax.all_gather(out_grad, "tensor", axis=0, tiled=True)
+    grad_all = joined_along(grow_blocks(out_grad, "tensor"), 0)
     grad_down = dot_tn(act, grad_all)
     grad_act = dot_nt(grad_all, wd)
     grad_gate = (grad_act * up * (sigma * (1.0 + gate * (1.0 - sigma)))).astype(jnp.bfloat16)

time: 1240 us -> 1200 us (0.968)
  waiting for transfers between devices: 873 us -> 830 us
  other arithmetic: 70.7 us -> 83.7 us
    ppermute x0 -> x3, waiting for transfers between devices: none -> 95.9 us  [grow_blocks(): other = lax.ppermute(blocks, axis, [(i, i ^ stride) for i in range(size)])]
    all_gather x1, waiting for transfers between devices: 77.6 us -> 0.01 us  [shards(): lax.all_gather(local[5], 'fsdp', axis=0, tiled=True)]
    all_gather x1 -> x0, waiting for transfers between devices: 41.6 us -> none  [shards(): grad_all = lax.all_gather(out_grad, 'tensor', axis=0, tiled=True)]
    all_gather x1, waiting for transfers between devices: 42.1 us -> 15.6 us  [shards(): lax.all_gather(normed_hidden.astype(jnp.bfloat16), 'tensor', axis=0, tile...]
  transfers between devices with their start and end apart: 22 -> 24, of which waited for: 21 -> 22; matrix products, arithmetic and copies ran while one was open for 21% -> 21% of each run, Pallas kernels for 0% -> 0%
where the time goes in v1:
time: 1200 us; the launch traced here: 1190 us
  waiting for transfers between devices  830 us (69%)
  matrix products  220 us (18%)
  other arithmetic  83.7 us (7%)
  blocking collectives  39.8 us (3%)
  between operations  15.1 us (1%)
    ppermute x3, waiting for transfers between devices, grow_blocks(): other = lax.ppermute(blocks, axis, [(i, i ^ stride) for i in range(size)])  95.9 us
    reduce_scatter x1, waiting for transfers between devices, shards(): lax.psum_scatter(jnp.dot(attended, wo, preferred_element_type=jnp.float32...  80.4 us
    reduce_scatter x1, waiting for transfers between devices, shards(): lax.psum_scatter(dot_nt(grad_gate, wg) + dot_nt(grad_up, wu), 'tensor', s...  80.2 us
    reduce_scatter x1, waiting for transfers between devices, shards(): lax.psum_scatter(grad_wgate.astype(jnp.bfloat16), 'fsdp', scatter_dimensi...  76.6 us
    all_gather x1, waiting for transfers between devices, shards(): lax.all_gather(local[4], 'fsdp', axis=0, tiled=True)  72 us
    all_gather x1, waiting for transfers between devices, shards(): lax.all_gather(local[6], 'fsdp', axis=1, tiled=True)  70.5 us
    reduce_scatter x1, waiting for transfers between devices, shards(): lax.psum_scatter(grad_na_part.astype(jnp.bfloat16), 'tensor', scatter_dim...  57.1 us
    dot_general x7, matrix products, dot_nt(): lax.dot_general(left, right, (((1,), (1,)), ((), ())), preferred_element_...  54.7 us
  transfers between devices with their start and end apart: 24, of which 22 were waited for; matrix products, arithmetic and copies ran while one was open for 21% of the time, Pallas kernels for 0%

profile of v1, /device:TPU:0, one launch (start us, length us, event | category | flops | bytes accessed | tf_op | source)
XLA Modules:
  0.0 1194.2 jit_solution(18056322508795903038)
XLA Ops:
  10.5 2.1 fusion.18
  17.1 1.8 fusion.7
  20.3 20.0 %all-gather.17.cloned.1.call-done = bf16[2048,256]{1,0:T(8,128)(2,1)} async-done(((bf16[512,256]{1,0:T(8,128)(2,1)}), bf16[2048,256]{1,0:T(8,128)(2,1)}) %all-gather.17.cloned.1.call-update) | async-done | bytes 1048592 | tf_op jit(solution)/shard_map/all_gather | solution.py:140
  40.3 43.0 %all-gather.11.cloned.1.call-done = bf16[1280,2048]{1,0:T(8,128)(2,1)} async-done(((bf16[160,2048]{1,0:T(8,128)(2,1)}), bf16[1280,2048]{1,0:T(8,128)(2,1)}) %all-gather.11.cloned.1.call-update) | async-done | bytes 5242896 | tf_op jit(solution)/shard_map/all_gather | solution.py:159
  83.3 4.3 fusion.43
  87.7 25.2 %all-gather.15.cloned.1.call-done = bf16[2048,256]{1,0:T(8,128)(2,1)} async-done(((bf16[512,256]{1,0:T(8,128)(2,1)}), bf16[2048,256]{1,0:T(8,128)(2,1)}) %all-gather.15.cloned.1.call-update) | async-done | bytes 1048592 | tf_op jit(solution)/shard_map/all_gather | solution.py:139
  112.9 4.3 fusion.42
  117.6 11.1 fusion.41
  128.7 10.6 fusion.1
  139.4 2.4 all-gather.13.cloned.1.call-done
  141.8 4.3 convolution_convert_fusion.9
  147.0 11.7 fusion.14
  158.7 12.0 %all-gather.19.cloned.1.call-done = bf16[256,2048]{1,0:T(8,128)(2,1)} async-done(((bf16[256,512]{1,0:T(8,128)(2,1)}), bf16[256,2048]{1,0:T(8,128)(2,1)}) %all-gather.19.cloned.1.call-update) | async-done | bytes 1048592 | tf_op jit(solution)/shard_map/all_gather | solution.py:142
  170.6 6.7 fusion.44
  178.2 80.4 %reduce-scatter.12.cloned.1.call-done = f32[160,2048]{1,0:T(8,128)} async-done(((f32[1280,2048]{1,0:T(8,128)}), f32[160,2048]{1,0:T(8,128)}) %reduce-scatter.12.cloned.1.call-update) | async-done | bytes 1310736 | tf_op jit(solution)/shard_map/reduce_scatter | solution.py:169
  262.1 2.1 collective-permute-done
  264.3 1.9 fusion.29
  267.6 29.7 %collective-permute-done.1 = bf16[2,160,2048]{2,1,0:T(8,128)(2,1)} collective-permute-done((bf16[2,160,2048]{2,1,0:T(8,128)(2,1)}, bf16[2,160,2048]{2,1,0:T(8,128)(2,1)}, u32[]{:S(2)}, u32[]{:S(2)}) %collective-permute-start.1) | collective-permute-done | bytes 1310752 | tf_op jit(solution)/shard_map/ppermute | solution.py:23
  297.3 2.0 pad_maximum_fusion.1
  299.3 2.1 reverse_select_fusion.1
  302.8 64.1 %collective-permute-done.2 = bf16[4,160,2048]{2,1,0:T(8,128)(2,1)} collective-permute-done((bf16[4,160,2048]{2,1,0:T(8,128)(2,1)}, bf16[4,160,2048]{2,1,0:T(8,128)(2,1)}, u32[]{:S(2)}, u32[]{:S(2)}) %collective-permute-start.2) | collective-permute-done | bytes 2621472 | tf_op jit(solution)/shard_map/ppermute | solution.py:23
  366.8 3.0 pad_maximum_fusion
  369.8 3.8 reverse_select_fusion
  373.7 15.6 %all-gather.21.cloned.1.call-done = bf16[1280,2048]{1,0:T(8,128)(2,1)} async-done(((bf16[160,2048]{1,0:T(8,128)(2,1)}), bf16[1280,2048]{1,0:T(8,128)(2,1)}) %all-gather.21.cloned.1.call-update) | async-done | bytes 5242896 | tf_op jit(solution)/shard_map/all_gather | solution.py:176
  389.3 10.4 fusion.46
  399.7 72.0 %all-gather.23.cloned.1.call-done = bf16[2048,1024]{1,0:T(8,128)(2,1)} async-done(((bf16[512,1024]{1,0:T(8,128)(2,1)}), bf16[2048,1024]{1,0:T(8,128)(2,1)}) %all-gather.23.cloned.1.call-update) | async-done | bytes 4194320 | tf_op jit(solution)/shard_map/all_gather | solution.py:143
  471.7 10.2 fusion.45
  481.9 70.5 %all-gather.27.cloned.1.call-done = bf16[1024,2048]{1,0:T(8,128)(2,1)} async-done(((bf16[1024,512]{1,0:T(8,128)(2,1)}), bf16[1024,2048]{1,0:T(8,128)(2,1)}) %all-gather.27.cloned.1.call-update) | async-done | bytes 4194320 | tf_op jit(solution)/shard_map/all_gather | solution.py:145
  552.4 14.6 %multiply_convert_fusion.1 = (bf16[1280,1024]{1,0:T(8,128)(2,1)S(1)}, bf16[1280,1024]{1,0:T(8,128)(2,1)S(1)}, bf16[1280,1024]{1,0:T(8,128)(2,1)}) fusion(f32[1280,1024]{1,0:T(8,128)} %fusion.45, f32[1280,1024]{1,0:T(8,128)} %fusion.46, bf16[1280,2048]{1,0:T(8,128)(2,1)} %bitcast.103, bf16[1024,2048]{1,0:T(8,128)(2,1)} %all-gather.27.cloned.1.call-done), kind=kOutput, calls=%fused_computation.19 | convolution fusion | flops 5388369920 | bytes 27787264 | tf_op jit(solution)/shard_map/dot_general | solution.py:31
  567.1 8.2 fusion.47
  575.3 10.9 convolution_add_fusion
  586.3 80.2 %reduce-scatter.16.cloned.1.call-done = f32[160,2048]{1,0:T(8,128)} async-done(((f32[1280,2048]{1,0:T(8,128)}), f32[160,2048]{1,0:T(8,128)}) %reduce-scatter.16.cloned.1.call-update) | async-done | bytes 1310736 | tf_op jit(solution)/shard_map/reduce_scatter | solution.py:204
  668.2 2.6 fusion.40
  670.9 10.1 convolution_convert_fusion.1
  681.1 10.2 convolution_convert_fusion.2
  691.3 10.2 convolution_convert_fusion.3
  702.0 10.1 all-gather.29.cloned.1.call-done
  712.1 5.0 convolution_convert_fusion.4
  717.2 4.0 convolution_convert_fusion.8
  721.2 10.8 fusion.11
  732.0 5.1 convolution_convert_fusion.5
  737.1 16.7 %multiply_reduce_fusion = (f32[4,1280]{1,0:T(4,128)S(1)}, f32[4,1280,1280]{1,2,0:T(8,128)}) fusion(f32[4,1280,1280]{1,2,0:T(8,128)} %get-tuple-element.93, f32[4,1280]{1,0:T(4,128)S(1)} %log_add_fusion, bf16[1280,4,64]{0,2,1:T(8,128)(2,1)S(1)} %bitcast.106, bf16[1280,4,64]{0,2,1:T(8,128)(2,1)S(1)} %bitcast.114), kind=kOutput, calls=%fused_computation.3 | convolution fusion | flops 858516480 | bytes 53780480 | tf_op jit(solution)/shard_map/while/body/eval_jaxpr/qhd,khd->hqk/dot_general | solution.py:109
  754.1 22.5 %multiply_convert_fusion = bf16[4,1280,1280]{1,2,0:T(8,128)(2,1)} fusion(f32[4,1280,1280]{1,2,0:T(8,128)} %get-tuple-element.95, f32[4,1280,1280]{1,2,0:T(8,128)} %get-tuple-element.93, f32[4,1280]{1,0:T(4,128)S(1)} %get-tuple-element.94, f32[4,1280]{1,0:T(4,128)S(1)} %log_add_fusion), kind=kLoop, calls=%fused_computation.2 | loop fusion | flops 26214400 | bytes 65576960 | tf_op jit(solution)/shard_map/while/body/eval_jaxpr/convert_element_type | solution.py:111
  776.6 9.0 fusion.10
  785.6 7.2 fusion.9
  793.3 2.6 convolution_convert_fusion.6
  796.0 5.1 convolution_convert_fusion.7
  801.4 2.9 fusion.48
  804.3 5.6 fusion.49
  809.9 8.4 add_convert_fusion
  818.3 10.0 convolution_convert_fusion
  828.4 2.9 convert_element_type.194
  831.2 39.5 %reduce-scatter.30.cloned.1.call-done = bf16[512,1024]{1,0:T(8,128)(2,1)} async-done(((bf16[2048,1024]{1,0:T(8,128)(2,1)}), bf16[512,1024]{1,0:T(8,128)(2,1)}) %reduce-scatter.30.cloned.1.call-update) | async-done | bytes 1048592 | tf_op jit(solution)/shard_map/reduce_scatter | solution.py:249
  870.8 2.8 convert_element_type.192
  873.5 76.6 %reduce-scatter.28.cloned.1.call-done = bf16[512,1024]{1,0:T(8,128)(2,1)} async-done(((bf16[2048,1024]{1,0:T(8,128)(2,1)}), bf16[512,1024]{1,0:T(8,128)(2,1)}) %reduce-scatter.28.cloned.1.call-update) | async-done | bytes 1048592 | tf_op jit(solution)/shard_map/reduce_scatter | solution.py:246
  950.2 2.8 convert_element_type.190
  953.0 27.2 %reduce-scatter.26.cloned.1.call-done = bf16[256,512]{1,0:T(8,128)(2,1)} async-done(((bf16[256,2048]{1,0:T(8,128)(2,1)}), bf16[256,512]{1,0:T(8,128)(2,1)}) %reduce-scatter.26.cloned.1.call-update) | async-done | bytes 262160 | tf_op jit(solution)/shard_map/reduce_scatter | solution.py:243
  981.9 26.1 %reduce-scatter.24.cloned.1.call-done = bf16[512,256]{1,0:T(8,128)(2,1)} async-done(((bf16[2048,256]{1,0:T(8,128)(2,1)}), bf16[512,256]{1,0:T(8,128)(2,1)}) %reduce-scatter.24.cloned.1.call-update) | async-done | bytes 262160 | tf_op jit(solution)/shard_map/reduce_scatter | solution.py:240
  1009.9 26.3 %reduce-scatter.22.cloned.1.call-done = bf16[512,256]{1,0:T(8,128)(2,1)} async-done(((bf16[2048,256]{1,0:T(8,128)(2,1)}), bf16[512,256]{1,0:T(8,128)(2,1)}) %reduce-scatter.22.cloned.1.call-update) | async-done | bytes 262160 | tf_op jit(solution)/shard_map/reduce_scatter | solution.py:237
  1038.0 26.3 %reduce-scatter.20.cloned.1.call-done = bf16[512,256]{1,0:T(8,128)(2,1)} async-done(((bf16[2048,256]{1,0:T(8,128)(2,1)}), bf16[512,256]{1,0:T(8,128)(2,1)}) %reduce-scatter.20.cloned.1.call-update) | async-done | bytes 262160 | tf_op jit(solution)/shard_map/reduce_scatter | solution.py:234
  1066.1 57.1 %reduce-scatter.18.cloned.1.call-done = bf16[160,2048]{1,0:T(8,128)(2,1)} async-done(((bf16[1280,2048]{1,0:T(8,128)(2,1)}), bf16[160,2048]{1,0:T(8,128)(2,1)}) %reduce-scatter.18.cloned.1.call-update) | async-done | bytes 655376 | tf_op jit(solution)/shard_map/reduce_scatter | solution.py:227
  1124.7 39.8 %all-reduce = (f32[2048]{0:T(1024)}, f32[2048]{0:T(1024)}) all-reduce(f32[2048]{0:T(1024)S(1)} %get-tuple-element.54, f32[2048]{0:T(1024)S(1)} %get-tuple-element.52), channel_id=1, replica_groups=mesh['fsdp'=4,'tensor'=8] {'fsdp','tensor'}, use_global_device_ids=true, to_apply=%region_14.15 | all-reduce | flops 4096 | bytes 32768 | tf_op jit(solution)/shard_map/psum | solution.py:232
  1164.4 19.3 %reduce-scatter.14.cloned.1.call-done = bf16[160,2048]{1,0:T(8,128)(2,1)} async-done(((bf16[1280,2048]{1,0:T(8,128)(2,1)}), bf16[160,2048]{1,0:T(8,128)(2,1)}) %reduce-scatter.14.cloned.1.call-update) | async-done | bytes 655376 | tf_op jit(solution)/shard_map/reduce_scatter | solution.py:182
  1183.8 3.4 fusion.23
  (146 shorter events, 29.6 us)
Async XLA Ops:
  7.2 33.1 %all-gather.17.cloned.1.call-start = ((), (), s32[]{:S(2)}) async-start(), calls=%async_computation.14 | async-start | bytes 1310720 | tf_op jit(solution)/shard_map/all_gather | solution.py:140
  7.9 75.4 %all-gather.11.cloned.1.call-start = ((), (), s32[]{:S(2)}) async-start(), calls=%async_computation.11 | async-start | bytes 5898240 | tf_op jit(solution)/shard_map/all_gather | solution.py:159
  8.6 1.3 copy-start.22
  10.0 0.6 copy-start.24
  12.7 100.2 %all-gather.15.cloned.1.call-start = ((), (), s32[]{:S(2)}) async-start(), calls=%async_computation.13 | async-start | bytes 1310720 | tf_op jit(solution)/shard_map/all_gather | solution.py:139
  13.4 128.3 %all-gather.13.cloned.1.call-start = ((), (), s32[]{:S(2)}) async-start(), calls=%async_computation.12 | async-start | bytes 1310720 | tf_op jit(solution)/shard_map/all_gather | solution.py:141
  14.0 156.6 %all-gather.19.cloned.1.call-start = ((), (), s32[]{:S(2)}) async-start(), calls=%async_computation.15 | async-start | bytes 1310720 | tf_op jit(solution)/shard_map/all_gather | solution.py:142
  14.6 243.9 %reduce-scatter.12.cloned.1.call-start = ((), (), s32[]{:S(2)}) async-start(), calls=%async_computation.16 | async-start | bytes 11796480 | tf_op jit(solution)/shard_map/reduce_scatter | solution.py:169
  20.2 97.0 %copy-start.4 = (f32[1280,32]{0,1:T(8,128)}, f32[1280,32]{0,1:T(8,128)S(1)}, u32[]{:S(2)}) copy-start(f32[1280,32]{0,1:T(8,128)S(1)} %get-tuple-element.91) | copy-start | bytes 491524
  117.6 11.1 copy-start.8
  117.6 11.1 copy-start.10
  117.6 11.1 copy-start.12
  117.6 11.1 copy-start.14
  146.1 0.8 copy-start.6
  158.7 18.7 %copy-start.19 = (bf16[4,64,1280]{2,1,0:T(8,128)(2,1)}, bf16[4,64,1280]{2,1,0:T(8,128)(2,1)S(1)}, u32[]{:S(2)}) copy-start(bf16[4,64,1280]{2,1,0:T(8,128)(2,1)S(1)} %fusion.14) | copy-start | bytes 1966084
  177.3 0.8 copy-start.26
  177.3 81.2 %copy-start = (bf16[160,2048]{1,0:T(8,128)(2,1)S(1)}, bf16[160,2048]{1,0:T(8,128)(2,1)}, u32[]{:S(2)}) copy-start(bf16[160,2048]{1,0:T(8,128)(2,1)} %param.12) | copy-start | bytes 1966084
  177.3 84.6 %copy-start.3 = (bf16[160,2048]{1,0:T(8,128)(2,1)S(1)}, bf16[160,2048]{1,0:T(8,128)(2,1)}, u32[]{:S(2)}) copy-start(bf16[160,2048]{1,0:T(8,128)(2,1)} %param.23) | copy-start | bytes 1966084
  177.4 196.3 %all-gather.25.cloned.1.call-start = ((), (), s32[]{:S(2)}) async-start(), calls=%async_computation.19 | async-start | bytes 5242880 | tf_op jit(solution)/shard_map/all_gather | solution.py:144
  178.1 211.2 %all-gather.21.cloned.1.call-start = ((), (), s32[]{:S(2)}) async-start(), calls=%async_computation.17 | async-start | bytes 5898240 | tf_op jit(solution)/shard_map/all_gather | solution.py:176
  261.2 210.5 %all-gather.23.cloned.1.call-start = ((), (), s32[]{:S(2)}) async-start(), calls=%async_computation.18 | async-start | bytes 5242880 | tf_op jit(solution)/shard_map/all_gather | solution.py:143
  261.9 290.5 %all-gather.27.cloned.1.call-start = ((), (), s32[]{:S(2)}) async-start(), calls=%async_computation.20 | async-start | bytes 5242880 | tf_op jit(solution)/shard_map/all_gather | solution.py:145
  262.0 2.2 collective-permute-start
  266.2 31.1 %collective-permute-start.1 = (bf16[2,160,2048]{2,1,0:T(8,128)(2,1)}, bf16[2,160,2048]{2,1,0:T(8,128)(2,1)}, u32[]{:S(2)}, u32[]{:S(2)}) collective-permute-start(bf16[2,160,2048]{2,1,0:T(8,128)(2,1)} %get-tuple-element.84), channel_id=1, source_target_pairs={{0,2},{1,3},{2,0},{3,1},{4,6},{5,7},{6,4},{7,5},{8,10},{9,11},{10,... | collective-permute-start | bytes 3932168 | tf_op jit(solution)/shard_map/ppermute | solution.py:23
  267.6 399.0 %reduce-scatter.16.cloned.1.call-start = ((), (), s32[]{:S(2)}) async-start(), calls=%async_computation.22 | async-start | bytes 11796480 | tf_op jit(solution)/shard_map/reduce_scatter | solution.py:204
  301.4 65.4 %collective-permute-start.2 = (bf16[4,160,2048]{2,1,0:T(8,128)(2,1)}, bf16[4,160,2048]{2,1,0:T(8,128)(2,1)}, u32[]{:S(2)}, u32[]{:S(2)}) collective-permute-start(bf16[4,160,2048]{2,1,0:T(8,128)(2,1)} %bitcast.18), channel_id=1, source_target_pairs={{0,4},{1,5},{2,6},{3,7},{4,0},{5,1},{6,2},{7,3},{8,12},{9,13},{10,... | collective-permute-start | bytes 7864328 | tf_op jit(solution)/shard_map/ppermute | solution.py:23
  552.4 14.7 %copy-start.28 = (bf16[2048,1024]{1,0:T(8,128)(2,1)S(1)}, bf16[2048,1024]{1,0:T(8,128)(2,1)}, u32[]{:S(2)}) copy-start(bf16[2048,1024]{1,0:T(8,128)(2,1)} %all-gather.23.cloned.1.call-done) | copy-start | bytes 12582916
  567.1 8.2 copy-start.30
  567.1 8.2 copy-start.29
  567.1 8.2 copy-start.27
  586.3 125.8 %all-gather.29.cloned.1.call-start = ((), (), s32[]{:S(2)}) async-start(), calls=%async_computation.23 | async-start | bytes 5898240 | tf_op jit(solution)/shard_map/all_gather | solution.py:210
  670.9 157.5 %reduce-scatter.32.cloned.1.call-start = ((), (), s32[]{:S(2)}) async-start(), calls=%async_computation.31 | async-start | bytes 5242880 | tf_op jit(solution)/shard_map/reduce_scatter | solution.py:252
  681.0 189.7 %reduce-scatter.30.cloned.1.call-start = ((), (), s32[]{:S(2)}) async-start(), calls=%async_computation.30 | async-start | bytes 5242880 | tf_op jit(solution)/shard_map/reduce_scatter | solution.py:249
  691.3 258.9 %reduce-scatter.28.cloned.1.call-start = ((), (), s32[]{:S(2)}) async-start(), calls=%async_computation.29 | async-start | bytes 5242880 | tf_op jit(solution)/shard_map/reduce_scatter | solution.py:246
  701.5 10.6 copy-start.20
  701.5 278.6 %reduce-scatter.26.cloned.1.call-start = ((), (), s32[]{:S(2)}) async-start(), calls=%async_computation.28 | async-start | bytes 1310720 | tf_op jit(solution)/shard_map/reduce_scatter | solution.py:243
  702.0 15.2 %copy-start.17 = (bf16[256,2048]{1,0:T(8,128)(2,1)S(1)}, bf16[256,2048]{1,0:T(8,128)(2,1)}, u32[]{:S(2)}) copy-start(bf16[256,2048]{1,0:T(8,128)(2,1)} %all-gather.19.cloned.1.call-done) | copy-start | bytes 3145732
  717.1 291.0 %reduce-scatter.24.cloned.1.call-start = ((), (), s32[]{:S(2)}) async-start(), calls=%async_computation.27 | async-start | bytes 1310720 | tf_op jit(solution)/shard_map/reduce_scatter | solution.py:240
  732.0 5.1 copy-start.7
  753.8 282.4 %reduce-scatter.22.cloned.1.call-start = ((), (), s32[]{:S(2)}) async-start(), calls=%async_computation.26 | async-start | bytes 1310720 | tf_op jit(solution)/shard_map/reduce_scatter | solution.py:237
  754.0 22.5 %copy-start.13 = (bf16[1280,4,32]{0,2,1:T(8,128)(2,1)S(1)}, bf16[1280,4,32]{0,2,1:T(8,128)(2,1)}, u32[]{:S(2)}) copy-start(bf16[1280,4,32]{0,2,1:T(8,128)(2,1)} %copy-done.12) | copy-start | bytes 983044
  754.1 22.5 %copy-start.15 = (bf16[1280,4,32]{0,2,1:T(8,128)(2,1)S(1)}, bf16[1280,4,32]{0,2,1:T(8,128)(2,1)}, u32[]{:S(2)}) copy-start(bf16[1280,4,32]{0,2,1:T(8,128)(2,1)} %copy-done.14) | copy-start | bytes 983044
  776.6 9.0 copy-start.9
  776.6 9.0 copy-start.11
  776.6 16.7 %slice-start = ((s8[5242880]{0:T(1024)(128)(4,1)}), s8[1048576]{0:T(1024)(128)(4,1)S(1)}, s32[]{:S(2)}) async-start(s8[5242880]{0:T(1024)(128)(4,1)} %bitcast.121), calls=%async_computation.32 | async-start | bytes 2097152
  785.6 7.3 copy-start.5
  785.6 7.3 copy-start.21
  785.6 7.7 slice-start.1
  795.9 268.3 %reduce-scatter.20.cloned.1.call-start = ((), (), s32[]{:S(2)}) async-start(), calls=%async_computation.25 | async-start | bytes 1310720 | tf_op jit(solution)/shard_map/reduce_scatter | solution.py:234
  801.1 322.1 %reduce-scatter.18.cloned.1.call-start = ((), (), s32[]{:S(2)}) async-start(), calls=%async_computation.24 | async-start | bytes 5898240 | tf_op jit(solution)/shard_map/reduce_scatter | solution.py:227
  801.4 2.9 copy-start.16
  804.3 5.6 copy-start.18
  818.3 365.5 %reduce-scatter.14.cloned.1.call-start = ((), (), s32[]{:S(2)}) async-start(), calls=%async_computation.21 | async-start | bytes 5898240 | tf_op jit(solution)/shard_map/reduce_scatter | solution.py:182
  831.2 291.9 %copy-start.1 = (bf16[160,2048]{1,0:T(8,128)(2,1)S(1)}, bf16[160,2048]{1,0:T(8,128)(2,1)}, u32[]{:S(2)}) copy-start(bf16[160,2048]{1,0:T(8,128)(2,1)} %param.12) | copy-start | bytes 1966084
  831.2 291.9 %copy-start.23 = (f32[2048]{0:T(1024)S(1)}, f32[2048]{0:T(1024)}, u32[]{:S(2)}) copy-start(f32[2048]{0:T(1024)} %copy-done.22) | copy-start | bytes 24580
  831.2 291.9 %copy-start.25 = (f32[160]{0:T(256)S(1)}, f32[160]{0:T(256)}, u32[]{:S(2)}) copy-start(f32[160]{0:T(256)} %copy-done.24) | copy-start | bytes 1924
  873.5 310.2 %copy-start.2 = (f32[160,2048]{1,0:T(8,128)S(1)}, f32[160,2048]{1,0:T(8,128)}, u32[]{:S(2)}) copy-start(f32[160,2048]{1,0:T(8,128)} %reduce-scatter.16.cloned.1.call-done) | copy-start | bytes 3932164
Sparse Core Ops, SparseCore 0:
  9.6 30.6 all-gather.16
  42.8 40.5 all-gather.10
  84.9 27.9 all-gather.14
  114.3 27.4 all-gather.12
  143.2 27.4 all-gather.18
  177.5 81.0 reduce-scatter.11
  260.1 80.7 all-gather.24
  343.3 45.9 all-gather.20
  390.9 80.7 all-gather.22
  473.1 79.2 all-gather.26
  586.4 80.0 reduce-scatter.15
  671.0 41.0 all-gather.28
  714.4 76.7 reduce-scatter.31
  793.5 77.2 reduce-scatter.29
  872.9 77.2 reduce-scatter.27
  952.4 27.6 reduce-scatter.25
  982.3 25.7 reduce-scatter.23
  1010.3 25.8 reduce-scatter.21
  1038.5 25.7 reduce-scatter.19
  1067.9 55.2 reduce-scatter.17
  1126.6 57.1 reduce-scatter.13
